TPU v7x, 32 devices: a whole 2x2x4 slice. The times are simulated.
32 devices in a mesh: row: 4 (over y, x), col: 8 (over z, core).
Axes of the slice: x: 2, y: 2, z: 4, core: 2. Of those that a mesh axis runs over, the one named last changes fastest.
Arguments:
- targets: float32 [2, 16384], P(None, ('row', 'col')), may hold values from 0 to 1
- sources: bfloat16 [2, 16384], P(None, 'col'), may hold values from 0 to 1
- omega: bfloat16 [256, 16384], P(None, 'col'), may hold values from -0.046875 to 0.046875
- tree_order: int32 [16384], P(('row', 'col')), may hold values from 0 to 16383, each once
- leaf_pivots: int32 [32, 128], P(('row', 'col')), may hold values from 0 to 511, all different within a row
- pivots_one: int32 [16, 128], replicated, may hold values from 0 to 255, all different within a row
- pivots_two: int32 [8, 128], replicated, may hold values from 0 to 255, all different within a row
- pivots_three: int32 [4, 128], replicated, may hold values from 0 to 255, all different within a row
Outputs:
- leaf_interp: float32 [16384, 128], P(('row', 'col'))
- level_one_interp: float32 [4096, 128], P(('row', 'col'))
- level_two_interp: float32 [2048, 128], P(('row', 'col'))
- level_three_interp: float32 [1024, 128], P(('row', 'col'))
- root_sketch: float32 [512, 256], P(('row', 'col'))
Inputs may be any that keep to these rules, and one draw needn't show every extreme that they name: tree_order names every target point once. `leaf_pivots`: each row names 128 distinct positions. `pivots_one`: each row names 128 distinct positions. `pivots_two`: each row names 128 distinct positions. `pivots_three`: each row names 128 distinct positions.
All inputs are finite; a program needn't handle non-finite values.
Results may differ from a plain program's by a relative error of at most 0.0074.
Values may be sent and summed in bfloat16 or wider, within the bound.
A program may use at most 192 MiB of HBM per device.

v0:
```python
import math
import jax
import jax.numpy as jnp
from jax import lax
from jax.sharding import PartitionSpec as P

LEAF = 512
S = 256
LEVELS = 3
RIDGE = 0.1
DELTA_SQUARED = 0.0001


def partner_2(block, axis, stride):
    count = lax.axis_size(axis)
    route = []
    for low in range(count):
        high = low | 1 << stride
        if high != low and high < count:
            route += [(low, high), (high, low)]
    return lax.ppermute(block, axis, route)


def kernel_block(points, source_pts):
    delta_x = points[0][:, None] - source_pts[0][None, :].astype(jnp.float32)
    delta_y = points[1][:, None] - source_pts[1][None, :].astype(jnp.float32)
    return (-0.5 * jnp.log(delta_x * delta_x + delta_y * delta_y + DELTA_SQUARED)).astype(
        jnp.bfloat16
    )


def select_factor(candidates, pivots):
    chosen = jnp.take(candidates, pivots, axis=0)
    gram_matrix = jnp.dot(chosen, chosen.T, precision=lax.Precision.HIGHEST)
    ridge_shift = RIDGE * (jnp.trace(gram_matrix) / chosen.shape[0] + 1e-06)
    shifted = gram_matrix + ridge_shift * jnp.eye(chosen.shape[0], dtype=gram_matrix.dtype)
    return (chosen, jnp.linalg.cholesky(shifted))


def solve_rows(chosen, factor, row_block):
    right_side = jnp.dot(chosen, row_block.T, precision=lax.Precision.HIGHEST)
    first = lax.linalg.triangular_solve(factor, right_side, left_side=True, lower=True)
    second = lax.linalg.triangular_solve(
        factor, first, left_side=True, lower=True, transpose_a=True
    )
    return second.T


def sketch_product(points, source_pts, weights):
    panel = kernel_block(points, source_pts)
    return lax.dot_general(
        panel, weights, (((1,), (1,)), ((), ())), preferred_element_type=jnp.float32
    )


def body(targets, sources, omega, tree_order, leaf_pivots, pivots_one, pivots_two, pivots_three):
    everyone = lax.all_gather(targets, ("row", "col"), axis=1, tiled=True)
    col_count = lax.axis_size("col")
    col_index = lax.axis_index("col")
    row_index = lax.axis_index("row")
    global_index = row_index * col_count + col_index
    positions = lax.all_gather(tree_order, "col", axis=0, tiled=True)
    placed = jnp.take(everyone, positions, axis=1)
    block_len = math.gcd(LEAF * lax.axis_size("col"), LEAF)
    blocks = placed.reshape(2, LEAF * lax.axis_size("col") // block_len, block_len).transpose(
        1, 0, 2
    )

    def one_block(points):
        return sketch_product(points, sources, omega)

    leaf_sketch = lax.psum_scatter(
        lax.map(one_block, blocks).reshape(LEAF * lax.axis_size("col"), S),
        "col",
        scatter_dimension=0,
        tiled=True,
    )
    chosen, factor = select_factor(leaf_sketch, leaf_pivots[0])
    results = [solve_rows(chosen, factor, leaf_sketch)]
    tables = (pivots_one, pivots_two, pivots_three)
    for section in range(LEVELS):
        partner = partner_2(chosen, "col", section)
        high_half = col_index >> section & 1 == 1
        candidates = jnp.where(
            high_half, jnp.concatenate([partner, chosen], 0), jnp.concatenate([chosen, partner], 0)
        )
        node_index = global_index >> section + 1
        node_pivots = lax.dynamic_index_in_dim(tables[section], node_index, 0, keepdims=False)
        group_size = 2 ** (section + 1)
        share_rows = candidates.shape[0] // group_size
        my_rows = lax.dynamic_slice_in_dim(
            candidates, col_index % group_size * share_rows, share_rows, 0
        )
        chosen, factor = select_factor(candidates, node_pivots)
        results.append(solve_rows(chosen, factor, my_rows))
    root_rows = chosen.shape[0] // 2**LEVELS
    root_share = lax.dynamic_slice_in_dim(chosen, col_index % 2**LEVELS * root_rows, root_rows, 0)
    return (results[0], results[1], results[2], results[3], root_share)


def solution(mesh):
    return jax.shard_map(
        body,
        mesh=mesh,
        in_specs=(
            P(None, ("row", "col")),
            P(None, "col"),
            P(None, "col"),
            P(("row", "col")),
            P(("row", "col"), None),
            P(),
            P(),
            P(),
        ),
        out_specs=(
            P(("row", "col"), None),
            P(("row", "col"), None),
            P(("row", "col"), None),
            P(("row", "col"), None),
            P(("row", "col"), None),
        ),
        check_vma=False,
    )
```

profile of v0, /device:TPU:0, one launch (start us, length us, event | category | flops | bytes accessed | tf_op | source)
XLA Modules:
  0.0 331.0 jit_solution(13750035460715798089)
XLA Ops:
  7.2 14.6 %all-gather = s32[8,1,512]{2,1,0:T(1,128)S(1)} all-gather(s32[1,1,512]{2,1,0:T(1,128)} %bitcast.123), channel_id=1, replica_groups=mesh['row'=4,'col'=8] {'col'}, dimensions={0}, use_global_device_ids=true | all-gather | bytes 18432 | tf_op jit(solution)/shard_map/all_gather | solution.py:62
  22.7 103.6 %all_gather.7 = f32[2,16384]{0,1:T(8,128)} all-gather(f32[2,512]{0,1:T(8,128)S(1)} %copy.23), channel_id=1, replica_groups=mesh['row'=4,'col'=8] {'row','col'}, dimensions={1}, use_global_device_ids=true | all-gather | bytes 135168 | tf_op jit(solution)/shard_map/all_gather | solution.py:57
  126.3 14.1 %gather_fusion = f32[4096,2]{1,0:T(8,128)S(1)} fusion(f32[2,16384]{0,1:T(8,128)} %all_gather.7, s32[4096]{0:T(1024)S(1)} %fusion.51), kind=kCustom, calls=%fused_computation.3 | custom fusion | bytes 81920 | tf_op jit(solution)/shard_map/jit(_take)/gather | solution.py:63
  141.2 18.9 %while.10 = (s32[]{:T(128)}, f32[8,512,256]{2,1,0:T(8,128)}, f32[8,2,512]{2,1,0:T(2,128)S(1)}, bf16[2,2048]{1,0:T(2,128)(2,1)S(1)}, bf16[256,2048]{1,0:T(8,128)(2,1)S(1)}, /*index=5*/s32[]{:T(128)}, s32[]{:T(128)}, s32[]{}) while((s32[]{:T(128)}, f32[8,512,256]{2,1,0:T(8,128)}, f32[8,2,512]{2,1,0:T(2,128)S(1)}, bf16[2,2048]{1,0:T(2,128)(2,1)S(1)}, ...), condition=%wide.region_1.2_spmd, body=%wide.region_0.1_spmd.sunk | while | flops 545263616 | bytes 1626729 | solution.py:73
  141.2 2.4 fusion.85
  143.6 2.4 fusion.85
  146.0 2.3 fusion.85
  148.4 2.3 fusion.85
  150.7 2.3 fusion.85
  153.1 2.3 fusion.85
  155.4 2.3 fusion.85
  157.8 2.3 fusion.85
  162.4 48.2 %reduce-scatter.2.cloned.1.call-done = f32[512,256]{1,0:T(8,128)} async-done(((f32[4096,256]{1,0:T(8,128)}), f32[512,256]{1,0:T(8,128)}) %reduce-scatter.2.cloned.1.call-update) | async-done | bytes 524304 | tf_op jit(solution)/shard_map/reduce_scatter | solution.py:72
  210.6 1.8 gather_fusion.1
  214.3 11.7 %cholesky.74 = f32[128,128]{1,0:T(8,128)S(1)} custom-call(f32[128,128]{1,0:T(8,128)S(1)} %copy.26), custom_call_target="Cholesky" | custom-call | tf_op jit(solution)/shard_map/jit(cholesky)/cholesky | solution.py:37
  227.4 9.8 %custom-call.22 = f32[1,128,128]{1,2,0:T(8,128)S(1)} custom-call(f32[1,128,128]{2,1,0:T(8,128)S(1)} %fusion.7), custom_call_target="InvertDiagBlocksLowerTriangular" | custom-call | tf_op jit(solution)/shard_map/triangular_solve | solution.py:43
  237.2 1.7 fusion.59
  243.4 11.9 %cholesky.85 = f32[128,128]{1,0:T(8,128)S(1)} custom-call(f32[128,128]{1,0:T(8,128)S(1)} %copy.28), custom_call_target="Cholesky" | custom-call | tf_op jit(solution)/shard_map/jit(cholesky)/cholesky | solution.py:37
  256.6 9.8 %custom-call.23 = f32[1,128,128]{1,2,0:T(8,128)S(1)} custom-call(f32[1,128,128]{2,1,0:T(8,128)S(1)} %fusion.8), custom_call_target="InvertDiagBlocksLowerTriangular" | custom-call | tf_op jit(solution)/shard_map/triangular_solve | solution.py:43
  268.8 1.5 collective-permute-start.2
  272.0 11.7 %cholesky.96 = f32[128,128]{1,0:T(8,128)S(1)} custom-call(f32[128,128]{1,0:T(8,128)S(1)} %copy.30), custom_call_target="Cholesky" | custom-call | tf_op jit(solution)/shard_map/jit(cholesky)/cholesky | solution.py:37
  285.1 9.8 %custom-call.24 = f32[1,128,128]{1,2,0:T(8,128)S(1)} custom-call(f32[1,128,128]{2,1,0:T(8,128)S(1)} %fusion.9), custom_call_target="InvertDiagBlocksLowerTriangular" | custom-call | tf_op jit(solution)/shard_map/triangular_solve | solution.py:43
  299.0 12.0 %cholesky.107 = f32[128,128]{1,0:T(8,128)S(1)} custom-call(f32[128,128]{1,0:T(8,128)S(1)} %copy.32), custom_call_target="Cholesky" | custom-call | tf_op jit(solution)/shard_map/jit(cholesky)/cholesky | solution.py:37
  312.3 9.8 %custom-call.25 = f32[1,128,128]{1,2,0:T(8,128)S(1)} custom-call(f32[1,128,128]{2,1,0:T(8,128)S(1)} %fusion.10), custom_call_target="InvertDiagBlocksLowerTriangular" | custom-call | tf_op jit(solution)/shard_map/triangular_solve | solution.py:43
  (99 shorter events, 23.1 us)
Async XLA Ops:
  7.2 203.4 %reduce-scatter.2.cloned.1.call-start = ((), (), s32[]{:S(2)}) async-start(), calls=%async_computation.1 | async-start | bytes 4718592 | tf_op jit(solution)/shard_map/reduce_scatter | solution.py:72
  22.7 118.5 %copy-start = (bf16[2,2048]{1,0:T(2,128)(2,1)S(1)}, bf16[2,2048]{1,0:T(2,128)(2,1)}, u32[]{:S(2)}) copy-start(bf16[2,2048]{1,0:T(2,128)(2,1)} %param.14) | copy-start | bytes 24580
  22.7 118.5 %copy-start.1 = (bf16[256,2048]{1,0:T(8,128)(2,1)S(1)}, bf16[256,2048]{1,0:T(8,128)(2,1)}, u32[]{:S(2)}) copy-start(bf16[256,2048]{1,0:T(8,128)(2,1)} %param.15) | copy-start | bytes 3145732
  160.1 2.2 copy-start.2
  212.5 28.1 %collective-permute-start = (f32[128,256]{1,0:T(8,128)S(1)}, f32[128,256]{1,0:T(8,128)S(1)}, u32[]{:S(2)}, u32[]{:S(2)}) collective-permute-start(f32[128,256]{1,0:T(8,128)S(1)} %broadcast_select_fusion.3), channel_id=1, source_target_pairs={{0,1},{1,0},{2,3},{3,2},{4,5},{5,4},{6,7},{7,6},{8,9},{9,8},{10,11... | collective-permute-start | bytes 393224 | tf_op jit(solution)/shard_map/ppermute | solution.py:21
  241.5 26.4 %collective-permute-start.1 = (f32[128,256]{1,0:T(8,128)S(1)}, f32[128,256]{1,0:T(8,128)S(1)}, u32[]{:S(2)}, u32[]{:S(2)}) collective-permute-start(f32[128,256]{1,0:T(8,128)S(1)} %broadcast_select_fusion.2), channel_id=1, source_target_pairs={{0,2},{2,0},{1,3},{3,1},{4,6},{6,4},{5,7},{7,5},{8,10},{10,8},{9,1... | collective-permute-start | bytes 393224 | tf_op jit(solution)/shard_map/ppermute | solution.py:21
  268.8 27.6 %collective-permute-start.2 = (f32[128,256]{1,0:T(8,128)S(1)}, f32[128,256]{1,0:T(8,128)S(1)}, u32[]{:S(2)}, u32[]{:S(2)}) collective-permute-start(f32[128,256]{1,0:T(8,128)S(1)} %broadcast_select_fusion.1), channel_id=1, source_target_pairs={{0,4},{4,0},{1,5},{5,1},{2,6},{6,2},{3,7},{7,3},{8,12},{12,8},{9,1... | collective-permute-start | bytes 393224 | tf_op jit(solution)/shard_map/ppermute | solution.py:21
Sparse Core Ops, SparseCore 0:
  160.3 50.2 reduce-scatter.1
where the time goes:
time: 331 us
  blocking collectives  118 us (36%)
  other arithmetic  94.6 us (29%)
  waiting for transfers between devices  48.2 us (15%)
  matrix products  29.9 us (9%)
  local copies, waits for them, and re-layouts  21.1 us (6%)
  between operations  17.1 us (5%)
    all_gather x1, blocking collectives, body(): everyone = lax.all_gather(targets, ('row', 'col'), axis=1, tiled=True)  104 us
    another operation x12, other arithmetic, select_factor(): return (chosen, jnp.linalg.cholesky(shifted))  50 us
    reduce_scatter x1, waiting for transfers between devices, body(): lax.psum_scatter(lax.map(one_block, blocks).reshape(LEAF * lax.axis_size(...  48.2 us
    another operation x8, other arithmetic, solve_rows(): lax.linalg.triangular_solve(factor, first, left_side=True, lower=True, tr...  41.9 us
    dot_general x8, matrix products, sketch_product(): lax.dot_general(panel, weights, (((1,), (1,)), ((), ())), preferred_eleme...  18.7 us
    gather x2, local copies, waits for them, and re-layouts, body(): placed = jnp.take(everyone, positions, axis=1)  14.8 us
    all_gather x1, blocking collectives, body(): positions = lax.all_gather(tree_order, 'col', axis=0, tiled=True)  14.6 us
  transfers between devices with their start and end apart: 4, of which 1 were waited for; matrix products, arithmetic and copies ran while one was open for 24% of the time, Pallas kernels for 0%

commit v1 on v0

--- a/solution.py
+++ b/solution.py
@@ -54,7 +54,7 @@
 
 
 def body(targets, sources, omega, tree_order, leaf_pivots, pivots_one, pivots_two, pivots_three):
-    everyone = lax.all_gather(targets, ("row", "col"), axis=1, tiled=True)
+    everyone = jnp.concatenate(lax.all_gather(targets, ("row", "col")), axis=1)
     col_count = lax.axis_size("col")
     col_index = lax.axis_index("col")
     row_index = lax.axis_index("row")

time: 331 us -> 269 us (0.81)
  blocking collectives: 118 us -> 55.6 us
  waiting for transfers between devices: 48.2 us -> 44.1 us
  local copies, waits for them, and re-layouts: 21.1 us -> 25.1 us
    all_gather x1, blocking collectives: 104 us -> 41 us  [body(): everyone = jnp.concatenate(lax.all_gather(targets, ('row', 'col')), axis=1)]
    reshape x0 -> x1, local copies, waits for them, and re-layouts: none -> 4.82 us  [body(): everyone = jnp.concatenate(lax.all_gather(targets, ('row', 'col')), axis=1)]
    reduce_scatter x1, waiting for transfers between devices: 48.2 us -> 44.1 us  [body(): lax.psum_scatter(lax.map(one_block, blocks).reshape(LEAF * lax.axis_size(...]
  transfers between devices with their start and end apart: 4 -> 4, of which waited for: 1 -> 1; matrix products, arithmetic and copies ran while one was open for 24% -> 30% of each run, Pallas kernels for 0% -> 0%
where the time goes in v1:
time: 269 us; the launch traced here: 268 us
  other arithmetic  94.7 us (35%)
  blocking collectives  55.6 us (21%)
  waiting for transfers between devices  44.1 us (16%)
  matrix products  29.9 us (11%)
  local copies, waits for them, and re-layouts  25.1 us (9%)
  between operations  17.1 us (6%)
    another operation x12, other arithmetic, select_factor(): return (chosen, jnp.linalg.cholesky(shifted))  50 us
    reduce_scatter x1, waiting for transfers between devices, body(): lax.psum_scatter(lax.map(one_block, blocks).reshape(LEAF * lax.axis_size(...  44.1 us
    another operation x8, other arithmetic, solve_rows(): lax.linalg.triangular_solve(factor, first, left_side=True, lower=True, tr...  41.9 us
    all_gather x1, blocking collectives, body(): everyone = jnp.concatenate(lax.all_gather(targets, ('row', 'col')), axis=1)  41 us
    dot_general x8, matrix products, sketch_product(): lax.dot_general(panel, weights, (((1,), (1,)), ((), ())), preferred_eleme...  18.7 us
    gather x2, local copies, waits for them, and re-layouts, body(): placed = jnp.take(everyone, positions, axis=1)  14.8 us
    all_gather x1, blocking collectives, body(): positions = lax.all_gather(tree_order, 'col', axis=0, tiled=True)  14.6 us
  transfers between devices with their start and end apart: 4, of which 1 were waited for; matrix products, arithmetic and copies ran while one was open for 30% of the time, Pallas kernels for 0%

profile of v1, /device:TPU:0, one launch (start us, length us, event | category | flops | bytes accessed | tf_op | source)
XLA Modules:
  0.0 268.3 jit_solution(9994639898182698676)
XLA Ops:
  7.2 14.6 %all-gather.1 = s32[8,1,512]{2,1,0:T(1,128)S(1)} all-gather(s32[1,1,512]{2,1,0:T(1,128)} %bitcast.129), channel_id=1, replica_groups=mesh['row'=4,'col'=8] {'col'}, dimensions={0}, use_global_device_ids=true | all-gather | bytes 18432 | tf_op jit(solution)/shard_map/all_gather | solution.py:62
  21.9 41.0 %all-gather.2 = f32[32,2,512]{2,1,0:T(2,128)S(1)} all-gather(f32[1,2,512]{2,1,0:T(2,128)} %bitcast.128), channel_id=2, replica_groups=mesh['row'=4,'col'=8] {'row','col'}, dimensions={0}, use_global_device_ids=true | all-gather | bytes 135168 | tf_op jit(solution)/shard_map/all_gather | solution.py:57
  62.9 4.8 %copy.23 = f32[2,32,512]{0,2,1:T(8,128)} copy(f32[2,32,512]{2,0,1:T(2,128)S(1)} %bitcast.121) | data formatting | bytes 262144 | tf_op jit(solution)/shard_map/reshape | solution.py:57
  67.7 14.1 %gather_fusion = f32[4096,2]{1,0:T(8,128)S(1)} fusion(f32[2,16384]{0,1:T(8,128)} %bitcast.118, s32[4096]{0:T(1024)S(1)} %fusion.51), kind=kCustom, calls=%fused_computation.3 | custom fusion | bytes 81920 | tf_op jit(solution)/shard_map/jit(_take)/gather | solution.py:63
  82.5 18.9 %while.10 = (s32[]{:T(128)}, f32[8,512,256]{2,1,0:T(8,128)}, f32[8,2,512]{2,1,0:T(2,128)S(1)}, bf16[2,2048]{1,0:T(2,128)(2,1)S(1)}, bf16[256,2048]{1,0:T(8,128)(2,1)S(1)}, /*index=5*/s32[]{:T(128)}, s32[]{:T(128)}, s32[]{}) while((s32[]{:T(128)}, f32[8,512,256]{2,1,0:T(8,128)}, f32[8,2,512]{2,1,0:T(2,128)S(1)}, bf16[2,2048]{1,0:T(2,128)(2,1)S(1)}, ...), condition=%wide.region_1.2_spmd, body=%wide.region_0.1_spmd.sunk | while | flops 545263616 | bytes 1626729 | solution.py:73
  82.6 2.4 fusion.85
  85.0 2.4 fusion.85
  87.4 2.3 fusion.85
  89.7 2.3 fusion.85
  92.1 2.3 fusion.85
  94.5 2.3 fusion.85
  96.8 2.3 fusion.85
  99.1 2.3 fusion.85
  103.7 44.1 %reduce-scatter.2.cloned.1.call-done = f32[512,256]{1,0:T(8,128)} async-done(((f32[4096,256]{1,0:T(8,128)}), f32[512,256]{1,0:T(8,128)}) %reduce-scatter.2.cloned.1.call-update) | async-done | bytes 524304 | tf_op jit(solution)/shard_map/reduce_scatter | solution.py:72
  147.8 1.8 gather_fusion.1
  151.6 11.7 %cholesky.74 = f32[128,128]{1,0:T(8,128)S(1)} custom-call(f32[128,128]{1,0:T(8,128)S(1)} %copy.26), custom_call_target="Cholesky" | custom-call | tf_op jit(solution)/shard_map/jit(cholesky)/cholesky | solution.py:37
  164.6 9.8 %custom-call.22 = f32[1,128,128]{1,2,0:T(8,128)S(1)} custom-call(f32[1,128,128]{2,1,0:T(8,128)S(1)} %fusion.7), custom_call_target="InvertDiagBlocksLowerTriangular" | custom-call | tf_op jit(solution)/shard_map/triangular_solve | solution.py:43
  174.5 1.7 fusion.59
  180.7 11.9 %cholesky.85 = f32[128,128]{1,0:T(8,128)S(1)} custom-call(f32[128,128]{1,0:T(8,128)S(1)} %copy.28), custom_call_target="Cholesky" | custom-call | tf_op jit(solution)/shard_map/jit(cholesky)/cholesky | solution.py:37
  193.9 9.8 %custom-call.23 = f32[1,128,128]{1,2,0:T(8,128)S(1)} custom-call(f32[1,128,128]{2,1,0:T(8,128)S(1)} %fusion.8), custom_call_target="InvertDiagBlocksLowerTriangular" | custom-call | tf_op jit(solution)/shard_map/triangular_solve | solution.py:43
  209.3 11.7 %cholesky.96 = f32[128,128]{1,0:T(8,128)S(1)} custom-call(f32[128,128]{1,0:T(8,128)S(1)} %copy.30), custom_call_target="Cholesky" | custom-call | tf_op jit(solution)/shard_map/jit(cholesky)/cholesky | solution.py:37
  222.3 9.8 %custom-call.24 = f32[1,128,128]{1,2,0:T(8,128)S(1)} custom-call(f32[1,128,128]{2,1,0:T(8,128)S(1)} %fusion.9), custom_call_target="InvertDiagBlocksLowerTriangular" | custom-call | tf_op jit(solution)/shard_map/triangular_solve | solution.py:43
  236.3 12.0 %cholesky.107 = f32[128,128]{1,0:T(8,128)S(1)} custom-call(f32[128,128]{1,0:T(8,128)S(1)} %copy.32), custom_call_target="Cholesky" | custom-call | tf_op jit(solution)/shard_map/jit(cholesky)/cholesky | solution.py:37
  249.6 9.8 %custom-call.25 = f32[1,128,128]{1,2,0:T(8,128)S(1)} custom-call(f32[1,128,128]{2,1,0:T(8,128)S(1)} %fusion.10), custom_call_target="InvertDiagBlocksLowerTriangular" | custom-call | tf_op jit(solution)/shard_map/triangular_solve | solution.py:43
  (99 shorter events, 23.7 us)
Async XLA Ops:
  7.2 140.7 %reduce-scatter.2.cloned.1.call-start = ((), (), s32[]{:S(2)}) async-start(), calls=%async_computation.1 | async-start | bytes 4718592 | tf_op jit(solution)/shard_map/reduce_scatter | solution.py:72
  62.9 19.7 %copy-start = (bf16[2,2048]{1,0:T(2,128)(2,1)S(1)}, bf16[2,2048]{1,0:T(2,128)(2,1)}, u32[]{:S(2)}) copy-start(bf16[2,2048]{1,0:T(2,128)(2,1)} %param.14) | copy-start | bytes 24580
  62.9 19.7 %copy-start.1 = (bf16[256,2048]{1,0:T(8,128)(2,1)S(1)}, bf16[256,2048]{1,0:T(8,128)(2,1)}, u32[]{:S(2)}) copy-start(bf16[256,2048]{1,0:T(8,128)(2,1)} %param.15) | copy-start | bytes 3145732
  101.5 2.2 copy-start.2
  149.7 28.1 %collective-permute-start = (f32[128,256]{1,0:T(8,128)S(1)}, f32[128,256]{1,0:T(8,128)S(1)}, u32[]{:S(2)}, u32[]{:S(2)}) collective-permute-start(f32[128,256]{1,0:T(8,128)S(1)} %broadcast_select_fusion.3), channel_id=1, source_target_pairs={{0,1},{1,0},{2,3},{3,2},{4,5},{5,4},{6,7},{7,6},{8,9},{9,8},{10,11... | collective-permute-start | bytes 393224 | tf_op jit(solution)/shard_map/ppermute | solution.py:21
  178.7 26.4 %collective-permute-start.1 = (f32[128,256]{1,0:T(8,128)S(1)}, f32[128,256]{1,0:T(8,128)S(1)}, u32[]{:S(2)}, u32[]{:S(2)}) collective-permute-start(f32[128,256]{1,0:T(8,128)S(1)} %broadcast_select_fusion.2), channel_id=1, source_target_pairs={{0,2},{2,0},{1,3},{3,1},{4,6},{6,4},{5,7},{7,5},{8,10},{10,8},{9,1... | collective-permute-start | bytes 393224 | tf_op jit(solution)/shard_map/ppermute | solution.py:21
  206.1 27.6 %collective-permute-start.2 = (f32[128,256]{1,0:T(8,128)S(1)}, f32[128,256]{1,0:T(8,128)S(1)}, u32[]{:S(2)}, u32[]{:S(2)}) collective-permute-start(f32[128,256]{1,0:T(8,128)S(1)} %broadcast_select_fusion.1), channel_id=1, source_target_pairs={{0,4},{4,0},{1,5},{5,1},{2,6},{6,2},{3,7},{7,3},{8,12},{12,8},{9,1... | collective-permute-start | bytes 393224 | tf_op jit(solution)/shard_map/ppermute | solution.py:21
Sparse Core Ops, SparseCore 0:
  101.6 46.1 reduce-scatter.1
